TPU v7x, 32 devices: a whole 2x2x4 slice. The times are simulated.
32 devices in a mesh: seq: 8 (over z, y), exp: 4 (over x, core).
Axes of the slice: x: 2, y: 2, z: 4, core: 2. Of those that a mesh axis runs over, the one named last changes fastest.
Arguments:
- projected: bfloat16 [4096, 3, 8192], P('seq', None, 'exp'), may hold values from -6 to 6
- log_decay: float32 [4096, 64], P('seq', 'exp'), may hold values from -2.5 to 0, as said below
- norm_gain: float32 [8192], P('exp'), may hold values from 0.1 to 1.9
- moe_tokens: bfloat16 [256, 6144], P(('seq', 'exp')), may hold values from -6 to 6
- expert_ids: int32 [256, 2], P(('seq', 'exp')), may hold values from 0 to 3, all different within a row; in each aligned block of 8 rows (0 to 7, 8 to 15, ...) at most 4 rows name the same one
- route_probs: float32 [256, 2], P(('seq', 'exp')), may hold values from 0.1 to 1
- w_in: bfloat16 [4, 6144, 2, 4608], P('exp', None, None, 'seq'), may hold values from -0.078125 to 0.078125
- w_out: bfloat16 [4, 4608, 6144], P('exp', 'seq'), may hold values from -0.09375 to 0.09375
Outputs:
- attn_out: bfloat16 [4096, 8192], P('seq', 'exp')
- moe_out: bfloat16 [256, 6144], P(('seq', 'exp'))
Inputs may be any that keep to these rules, and one draw needn't show every extreme that they name: `log_decay`: negative in every entry. `expert_ids`: A token names 2 different experts. In the rows of one device (aligned blocks of 8 tokens) no expert is named more than 4 times, a bound that some block reaches.
All inputs are finite; a program needn't handle non-finite values.
Results may differ from a plain program's by a relative error of at most 0.025.
Values may be sent and summed in bfloat16 or wider, within the bound.
No kernel may reach another device: no remote copies, remote signals or barrier semaphores. Data moves between devices by JAX's collectives and lax.ppermute only.
A program may use at most 128 MiB of HBM per device.

v0:
```python
import jax
import jax.numpy as jnp
from jax import lax
from jax.sharding import PartitionSpec as P

CAP = 4
EPS = 1e-06
HIGH = lax.Precision.HIGHEST


def prefix(shard, axis, join, neutral):
    place = lax.axis_index(axis)
    gathered = jax.tree.map(
        lambda a, kind: lax.all_gather(a.astype(kind), axis), shard, (jnp.bfloat16, jnp.bfloat16)
    )
    state = jax.tree.map(lambda a, e: jnp.zeros_like(a) + jnp.asarray(e, a.dtype), shard, neutral)

    def one(turn, state):
        return join(
            state,
            jax.tree.map(
                lambda a, own: lax.dynamic_index_in_dim(a, turn, 0, False).astype(own.dtype),
                gathered,
                shard,
            ),
        )

    return lax.fori_loop(0, place, one, state)


def combine_states(earlier, later):
    return (earlier[0] * later[0], later[0][:, None, None] * earlier[1] + later[1])


def on_device(projected, log_decay, norm_gain, moe_tokens, expert_ids, route_probs, w_in, w_out):
    rows = projected.shape[0]
    heads = log_decay.shape[1]
    width = projected.shape[2] // heads
    queries = projected[:, 0].reshape(rows, heads, width)
    key_rows = projected[:, 1].reshape(rows, heads, width)
    values = projected[:, 2].reshape(rows, heads, width)
    running = jnp.cumsum(log_decay, axis=0)
    last = running[-1]
    weighted = key_rows.astype(jnp.float32) * jnp.exp(last[None] - running)[:, :, None]
    block_state = jnp.einsum("thi,thj->hij", weighted, values.astype(jnp.float32), precision=HIGH)
    identity = (jnp.ones_like(last), jnp.zeros_like(block_state))
    _, carried = prefix((jnp.exp(last), block_state), "seq", combine_states, identity)
    scores = jnp.einsum("thd,uhd->htu", queries, key_rows, preferred_element_type=jnp.float32)
    turned = running.T
    gap = turned[:, :, None] - turned[:, None, :]
    causal = (jnp.arange(rows)[:, None] >= jnp.arange(rows)[None, :])[None]
    decay = jnp.exp(jnp.where(causal, gap, -jnp.inf))
    weights = (scores * decay).astype(jnp.bfloat16)
    local_part = jnp.einsum("htu,uhd->thd", weights, values, preferred_element_type=jnp.float32)
    carried_part = jnp.einsum(
        "thd,hde->the",
        queries.astype(jnp.float32) * jnp.exp(running)[:, :, None],
        carried,
        precision=HIGH,
    )
    mixed = local_part + carried_part
    scaled = mixed * lax.rsqrt(jnp.mean(mixed * mixed, axis=-1, keepdims=True) + EPS)
    attn_out = (scaled.reshape(rows, heads * width) * norm_gain).astype(jnp.bfloat16)
    count_tok = moe_tokens.shape[0]
    model_width = moe_tokens.shape[1]
    topk = expert_ids.shape[1]
    experts = w_in.shape[0] * lax.axis_size("exp")
    assigned = expert_ids.reshape(-1)
    onehot = (assigned[:, None] == jnp.arange(experts, dtype=jnp.int32)[None]).astype(jnp.int32)
    slot = jnp.sum((jnp.cumsum(onehot, axis=0) - onehot) * onehot, axis=1)
    target = assigned * CAP + slot
    pick = (target[None, :] == jnp.arange(experts * CAP, dtype=jnp.int32)[:, None]).astype(
        jnp.bfloat16
    )
    local_units = w_in.shape[3]
    joined_in = w_in.reshape(model_width, 2 * local_units)
    down = w_out[0]
    spread_rows = jnp.repeat(moe_tokens, topk, axis=0)
    outgoing = (
        jnp.dot(pick, spread_rows, preferred_element_type=jnp.float32)
        .astype(jnp.bfloat16)
        .reshape(experts, CAP, model_width)
    )
    arrived = lax.all_to_all(outgoing, "exp", split_axis=0, concat_axis=0, tiled=True)
    both = jnp.dot(
        lax.all_gather(arrived.reshape(experts * CAP, model_width), "seq", axis=0, tiled=True),
        joined_in,
        preferred_element_type=jnp.float32,
    )
    hidden = (jax.nn.silu(both[:, :local_units]) * both[:, local_units:]).astype(jnp.bfloat16)
    summed = lax.psum_scatter(
        jnp.dot(hidden, down, preferred_element_type=jnp.float32).astype(jnp.bfloat16),
        "seq",
        scatter_dimension=0,
        tiled=True,
    )
    results = summed.reshape(experts, CAP, model_width)
    returned = lax.all_to_all(results, "exp", split_axis=0, concat_axis=0, tiled=True)
    picked = jnp.dot(
        pick.T, returned.reshape(experts * CAP, model_width), preferred_element_type=jnp.float32
    )
    scaled_rows = picked * route_probs.reshape(-1)[:, None]
    moe_out = jnp.sum(scaled_rows.reshape(count_tok, topk, model_width), axis=1).astype(
        jnp.bfloat16
    )
    return (attn_out, moe_out)


def solution(mesh):
    in_specs = (
        P("seq", None, "exp"),
        P("seq", "exp"),
        P("exp"),
        P(("seq", "exp"), None),
        P(("seq", "exp"), None),
        P(("seq", "exp"), None),
        P("exp", None, None, "seq"),
        P("exp", "seq", None),
    )
    out_specs = (P("seq", "exp"), P(("seq", "exp"), None))
    return jax.shard_map(
        on_device, mesh=mesh, in_specs=in_specs, out_specs=out_specs, check_vma=False
    )
```

profile of v0, /device:TPU:31, one launch (start us, length us, event | category | flops | bytes accessed | tf_op | source)
XLA Modules:
  0.0 248.3 jit_solution(5509535321156864374)
XLA Ops:
  7.2 0.0 copy-start
  7.2 0.0 all-gather.5.cloned.1.call-start
  7.2 0.8 copy.66
  8.0 0.1 reshape.107
  8.1 0.1 fusion.18
  8.2 0.2 select_reduce_fusion
  8.4 1.0 broadcast_in_dim.21
  9.4 0.1 reshape.108
  9.5 0.2 convolution_convert_fusion.1
  9.7 0.1 reshape.109
  9.7 6.6 %all_to_all.10 = bf16[4,4,6144]{2,1,0:T(4,128)(2,1)S(1)} all-to-all(bf16[4,4,6144]{2,1,0:T(4,128)(2,1)S(1)} %reshape.109), channel_id=1, replica_groups=mesh['seq'=8,'exp'=4] {'exp'}, dimensions={0} | all-to-all | bytes 393216 | tf_op jit(solution)/shard_map/all_to_all | solution.py:84
  16.3 0.7 reshape.110
  17.0 0.0 all-gather.5.cloned.1.call-update
  17.1 0.0 reduce-scatter.2.cloned.1.call-start
  17.1 43.5 %all-gather.5.cloned.1.call-done = bf16[128,6144]{1,0:T(8,128)(2,1)} async-done(((bf16[16,6144]{1,0:T(8,128)(2,1)}), bf16[128,6144]{1,0:T(8,128)(2,1)}) %all-gather.5.cloned.1.call-update) | async-done | bytes 1572880 | tf_op jit(solution)/shard_map/all_gather | solution.py:86
  60.6 10.1 %fusion.26 = f32[128,1152]{1,0:T(8,128)S(1)} fusion(bf16[128,6144]{1,0:T(8,128)(2,1)} %all-gather.5.cloned.1.call-done, bf16[6144,1152]{0,1:T(8,128)(2,1)} %bitcast.59), kind=kOutput, calls=%fused_computation.47 | convolution fusion | flops 1811939328 | bytes 16318464 | tf_op jit(solution)/shard_map/dot_general | solution.py:85
  70.8 5.6 %convolution_convert_fusion = bf16[128,6144]{1,0:T(8,128)(2,1)} fusion(bf16[1,576,6144]{2,1,0:T(8,128)(2,1)} %param.17, f32[128,1152]{1,0:T(8,128)S(1)} %fusion.26), kind=kOutput, calls=%fused_computation.3 | convolution fusion | flops 907198464 | bytes 9306112 | tf_op jit(solution)/shard_map/dot_general | solution.py:92
  76.4 0.0 reduce-scatter.2.cloned.1.call-update
  76.4 0.0 all-gather.7.cloned.1.call-start
  76.4 0.0 copy-done
  76.5 1.2 reduce-window.6
  77.6 0.2 slice_reduce_fusion
  77.8 5.8 %fusion.25 = (bf16[512,1,2048]{2,0,1:T(8,128)(2,1)}, bf16[512,1,2048]{2,0,1:T(8,128)(2,1)}, bf16[512,1,2048]{2,0,1:T(8,128)(2,1)S(1)}) fusion(bf16[512,3,2048]{2,0,1:T(8,128)(2,1)} %param.10), kind=kLoop, calls=%fused_computation.46 | loop fusion | bytes 12582912 | tf_op jit(solution)/shard_map/slice | solution.py:40
  83.7 3.9 %copy.75 = bf16[512,1,2048]{0,2,1:T(8,128)(2,1)} copy(bf16[512,1,2048]{2,0,1:T(8,128)(2,1)} %get-tuple-element.57) | data formatting | bytes 4194304
  87.6 2.5 %copy.61 = bf16[512,1,2048]{0,2,1:T(8,128)(2,1)} copy(bf16[512,1,2048]{2,0,1:T(8,128)(2,1)S(1)} %get-tuple-element.59) | data formatting | bytes 4194304 | tf_op jit(solution)/shard_map/slice | solution.py:41
  90.1 0.1 fusion.24
  90.2 0.2 slice_reduce_fusion.1
  90.3 0.1 bitcast_exponential_fusion
  90.5 5.3 %fusion.12 = bf16[16,128,128]{2,1,0:T(8,128)(2,1)} fusion(bf16[512,16,128]{0,2,1:T(8,128)(2,1)} %bitcast.64, bf16[512,16,128]{0,2,1:T(8,128)(2,1)} %bitcast.62, f32[512,16]{0,1:T(8,128)S(1)} %get-tuple-element.61), kind=kOutput, calls=%fused_computation.20 | convolution fusion | flops 1612972032 | bytes 4751360 | tf_op jit(solution)/shard_map/thi,thj->hij/dot_general | solution.py:45
  95.7 0.0 all-gather.7.cloned.1.call-update
  95.8 2.9 %copy.74 = bf16[512,1,2048]{0,2,1:T(8,128)(2,1)S(1)} copy(bf16[512,1,2048]{2,0,1:T(8,128)(2,1)} %get-tuple-element.58) | data formatting | bytes 4194304
  98.6 0.1 iota_compare_fusion
  98.7 40.0 %reduce-scatter.2.cloned.1.call-done = bf16[16,6144]{1,0:T(8,128)(2,1)} async-done(((bf16[128,6144]{1,0:T(8,128)(2,1)}), bf16[16,6144]{1,0:T(8,128)(2,1)}) %reduce-scatter.2.cloned.1.call-update) | async-done | bytes 196624 | tf_op jit(solution)/shard_map/reduce_scatter | solution.py:91
  138.7 1.7 reshape.112
  140.4 5.7 %all-to-all-start.1 = ((bf16[4,4,6144]{2,1,0:T(4,128)(2,1)}), bf16[4,4,6144]{2,1,0:T(4,128)(2,1)S(1)}, u32[]{:S(2)}, u32[]{:S(2)}) async-start(bf16[4,4,6144]{2,1,0:T(4,128)(2,1)} %reshape.112), calls=%async_computation.2 | async-start | bytes 393216 | tf_op jit(solution)/shard_map/all_to_all | solution.py:98
  146.2 0.0 copy-start.3
  146.2 10.7 %fusion.11 = f32[16,512,128]{1,2,0:T(8,128)} fusion(bf16[512,16,128]{0,2,1:T(8,128)(2,1)} %bitcast.65, bf16[512,16,128]{0,2,1:T(8,128)(2,1)S(1)} %bitcast.60, bf16[512,16,128]{0,2,1:T(8,128)(2,1)} %bitcast.63, f32[16,512]{1,0:T(8,128)S(1)} %get-tuple-element.63, pred[512,512]{1,0:T(8,128)(4,1)S(1)} %iota_compare_fusion), kind=kOutput, calls=%fused_computation.19 | convolution fusion | flops 2164260864 | bytes 10780672 | tf_op jit(solution)/shard_map/htu,uhd->thd/dot_general | solution.py:54
  156.8 0.2 fusion.19
  157.0 13.0 %all-gather.1 = bf16[8,1,16]{2,1,0:T(2,128)(2,1)S(1)} all-gather(bf16[1,1,16]{2,1,0:T(2,128)(2,1)S(1)} %bitcast.68), channel_id=1, replica_groups=mesh['seq'=8,'exp'=4] {'seq'}, dimensions={0}, use_global_device_ids=true | all-gather | bytes 288 | tf_op jit(solution)/shard_map/all_gather | solution.py:14
  170.1 0.0 copy-done.3
  170.1 0.1 copy.67
  170.1 0.1 mul.92
  170.2 0.0 all-to-all-done.1
  170.3 0.3 convolution_multiply_fusion
  170.6 0.2 reshape.114
  170.8 1.1 reduce_sum.29
  171.9 42.6 %all-gather.7.cloned.1.call-done = bf16[128,128,128]{2,1,0:T(8,128)(2,1)} async-done(((bf16[16,128,128]{2,1,0:T(8,128)(2,1)}), bf16[128,128,128]{2,1,0:T(8,128)(2,1)}) %all-gather.7.cloned.1.call-update) | async-done | bytes 4194320 | tf_op jit(solution)/shard_map/all_gather | solution.py:14
  214.5 0.1 broadcast_in_dim.20
  214.6 9.4 %while.12 = (s32[]{:T(128)}, f32[16,128,128]{2,1,0:T(8,128)S(1)}, s32[]{:T(128)}, bf16[8,16]{1,0:T(8,128)(2,1)S(1)}, bf16[8,16,128,128]{3,2,1,0:T(8,128)(2,1)}, /*index=5*/s32[]{:T(128)}, s32[]{:T(128)}, s32[]{:T(128)}) while((s32[]{:T(128)}, f32[16,128,128]{2,1,0:T(8,128)S(1)}, s32[]{:T(128)}, bf16[8,16]{1,0:T(8,128)(2,1)S(1)}, ...), condition=%wide.region_3.4_spmd, body=%wide.region_2.3_spmd.sunk | while | flops 786453 | bytes 2621727 | solution.py:28
  214.6 1.3 convert_add_fusion.2
  216.0 1.3 convert_add_fusion.2
  217.3 1.3 convert_add_fusion.2
  218.7 1.3 convert_add_fusion.2
  220.0 1.3 convert_add_fusion.2
  221.4 1.3 convert_add_fusion.2
  222.7 1.3 convert_add_fusion.2
  224.0 5.8 %multiply_reduce_fusion = (f32[512,16]{0,1:T(8,128)S(1)}, f32[512,16,128]{0,2,1:T(8,128)S(1)}) fusion(f32[16,128,128]{2,1,0:T(8,128)S(1)} %get-tuple-element.46, bf16[512,16,128]{0,2,1:T(8,128)(2,1)S(1)} %bitcast.61, f32[512,16]{0,1:T(8,128)S(1)} %get-tuple-element.60, f32[16,512,128]{1,2,0:T(8,128)} %fusion.11), kind=kOutput, calls=%fused_computation.9 | convolution fusion | flops 1615847424 | bytes 11599872 | tf_op jit(solution)/shard_map/thd,hde->the/dot_general | solution.py:55
  229.8 2.5 %broadcast_multiply_fusion = f32[512,16,128]{0,2,1:T(8,128)} fusion(f32[512,16,128]{0,2,1:T(8,128)S(1)} %get-tuple-element.65, f32[512,16]{0,1:T(8,128)S(1)} %add_rsqrt_fusion), kind=kLoop, calls=%fused_computation.16 | loop fusion | flops 1048576 | bytes 8421376 | tf_op jit(solution)/shard_map/mul | solution.py:62
  232.3 0.0 copy-start.2
  232.3 0.0 copy-start.1
  232.3 5.4 %copy.65 = f32[512,2048]{1,0:T(8,128)} copy(f32[512,2048]{0,1:T(8,128)} %bitcast.58) | data formatting | bytes 8388608 | tf_op jit(solution)/shard_map/reshape | solution.py:63
  237.8 0.0 copy-done.2
  237.8 4.0 %multiply_convert_fusion.1 = bf16[512,2048]{1,0:T(8,128)(2,1)} fusion(f32[512,2048]{1,0:T(8,128)} %copy.65, f32[2048]{0:T(1024)S(1)} %copy-done.2), kind=kLoop, calls=%fused_computation.8 | loop fusion | flops 2097152 | bytes 6299648 | tf_op jit(solution)/shard_map/convert_element_type | solution.py:63
  241.8 0.0 copy-done.1
  (15 shorter events, 0.2 us)
Async XLA Ops:
  7.2 69.3 %copy-start = (f32[512,16]{0,1:T(8,128)S(1)}, f32[512,16]{0,1:T(8,128)}, u32[]{:S(2)}) copy-start(f32[512,16]{0,1:T(8,128)} %param.11) | copy-start | bytes 98308
  7.2 53.4 %all-gather.5.cloned.1.call-start = ((), (), s32[]{:S(2)}) async-start(), calls=%async_computation.3 | async-start | bytes 1769472 | tf_op jit(solution)/shard_map/all_gather | solution.py:86
  17.1 121.7 %reduce-scatter.2.cloned.1.call-start = ((), (), s32[]{:S(2)}) async-start(), calls=%async_computation.4 | async-start | bytes 1769472 | tf_op jit(solution)/shard_map/reduce_scatter | solution.py:91
  76.4 138.1 %all-gather.7.cloned.1.call-start = ((), (), s32[]{:S(2)}) async-start(), calls=%async_computation.5 | async-start | bytes 4718592 | tf_op jit(solution)/shard_map/all_gather | solution.py:14
  140.4 29.8 %all-to-all-start.1 = ((bf16[4,4,6144]{2,1,0:T(4,128)(2,1)}), bf16[4,4,6144]{2,1,0:T(4,128)(2,1)S(1)}, u32[]{:S(2)}, u32[]{:S(2)}) async-start(bf16[4,4,6144]{2,1,0:T(4,128)(2,1)} %reshape.112), calls=%async_computation.2 | async-start | bytes 393216 | tf_op jit(solution)/shard_map/all_to_all | solution.py:98
  146.2 23.9 %copy-start.3 = (f32[8,2]{0,1:T(2,128)S(1)}, f32[8,2]{0,1:T(2,128)}, u32[]{:S(2)}) copy-start(f32[8,2]{0,1:T(2,128)} %param.15) | copy-start | bytes 196
  232.3 5.4 %copy-start.2 = (f32[2048]{0:T(1024)S(1)}, f32[2048]{0:T(1024)}, u32[]{:S(2)}) copy-start(f32[2048]{0:T(1024)} %param.12) | copy-start | bytes 24580
  232.3 9.4 %copy-start.1 = (f32[512,16]{0,1:T(8,128)S(1)}, f32[512,16]{0,1:T(8,128)}, u32[]{:S(2)}) copy-start(f32[512,16]{0,1:T(8,128)} %param.11) | copy-start | bytes 98308
Sparse Core Ops, SparseCore 0:
  17.2 43.3 all-gather.4
  76.5 62.1 reduce-scatter.1
  141.1 73.3 all-gather.6
where the time goes:
time: 249 us; the launch traced here: 248 us
  waiting for transfers between devices  126 us (51%)
  matrix products  37.9 us (15%)
  local copies, waits for them, and re-layouts  25.9 us (10%)
  blocking collectives  19.6 us (8%)
  other arithmetic  18.7 us (8%)
  between operations  13.9 us (6%)
  starting transfers between devices  5.84 us (2%)
    all_gather x1, waiting for transfers between devices, on_device(): lax.all_gather(arrived.reshape(experts * CAP, model_width), 'seq', axis=0...  43.5 us
    all_gather x1, waiting for transfers between devices, prefix(): lax.all_gather(a.astype(kind), axis)  42.6 us
    reduce_scatter x1, waiting for transfers between devices, on_device(): lax.psum_scatter(jnp.dot(hidden, down, preferred_element_type=jnp.float32...  40 us
    all_gather x1, blocking collectives, prefix(): lax.all_gather(a.astype(kind), axis)  13 us
    dot_general x1, matrix products, on_device(): jnp.einsum('htu,uhd->thd', weights, values, preferred_element_type=jnp.fl...  10.7 us
    dot_general x1, matrix products, on_device(): jnp.dot(lax.all_gather(arrived.reshape(experts * CAP, model_width), 'seq'...  10.1 us
    add x7, other arithmetic, combine_states(): later[0][:, None, None] * earlier[1] + later[1]  9.08 us
    unnamed x13, local copies, waits for them, and re-layouts  7.68 us
  transfers between devices with their start and end apart: 4, of which 3 were waited for; matrix products, arithmetic and copies ran while one was open for 15% of the time, Pallas kernels for 0%

commit v1 on v0

--- a/solution.py
+++ b/solution.py
@@ -6,6 +6,18 @@
 CAP = 4
 EPS = 1e-06
 HIGH = lax.Precision.HIGHEST
+
+
+def doubled_up(x, axis, dim):
+    ways, here, step = (lax.axis_size(axis), lax.axis_index(axis), x.shape[dim])
+    line, have = (x, 1)
+    while have < ways:
+        line = jnp.concatenate(
+            [line, lax.ppermute(line, axis, [(d, (d - have) % ways) for d in range(ways)])],
+            axis=dim,
+        )
+        have = 2 * have
+    return jnp.roll(line, here * step, axis=dim)
 
 
 def prefix(shard, axis, join, neutral):
@@ -83,7 +95,7 @@
     )
     arrived = lax.all_to_all(outgoing, "exp", split_axis=0, concat_axis=0, tiled=True)
     both = jnp.dot(
-        lax.all_gather(arrived.reshape(experts * CAP, model_width), "seq", axis=0, tiled=True),
+        doubled_up(arrived.reshape(experts * CAP, model_width), "seq", 0),
         joined_in,
         preferred_element_type=jnp.float32,
     )

time: 249 us -> 260 us (1.044)
  waiting for transfers between devices: 126 us -> 137 us
    ppermute x0 -> x3, waiting for transfers between devices: none -> 54.3 us  [doubled_up(): lax.ppermute(line, axis, [(d, (d - have) % ways) for d in range(ways)])]
    all_gather x1 -> x0, waiting for transfers between devices: 43.5 us -> none  [on_device(): lax.all_gather(arrived.reshape(experts * CAP, model_width), 'seq', axis=0...]
    unnamed x13 -> x20, local copies, waits for them, and re-layouts: 7.68 us -> 6.41 us
  transfers between devices with their start and end apart: 4 -> 6, of which waited for: 3 -> 5; matrix products, arithmetic and copies ran while one was open for 15% -> 14% of each run, Pallas kernels for 0% -> 0%
where the time goes in v1:
time: 260 us; the launch traced here: 259 us
  waiting for transfers between devices  137 us (53%)
  matrix products  37.5 us (14%)
  local copies, waits for them, and re-layouts  25.4 us (10%)
  blocking collectives  19.6 us (8%)
  other arithmetic  18.8 us (7%)
  between operations  14.3 us (6%)
  starting transfers between devices  6.19 us (2%)
    ppermute x3, waiting for transfers between devices, doubled_up(): lax.ppermute(line, axis, [(d, (d - have) % ways) for d in range(ways)])  54.3 us
    all_gather x1, waiting for transfers between devices, prefix(): lax.all_gather(a.astype(kind), axis)  42.6 us
    reduce_scatter x1, waiting for transfers between devices, on_device(): lax.psum_scatter(jnp.dot(hidden, down, preferred_element_type=jnp.float32...  40.3 us
    all_gather x1, blocking collectives, prefix(): lax.all_gather(a.astype(kind), axis)  13.1 us
    dot_general x1, matrix products, on_device(): jnp.einsum('htu,uhd->thd', weights, values, preferred_element_type=jnp.fl...  10.7 us
    dot_general x1, matrix products, on_device(): jnp.dot(doubled_up(arrived.reshape(experts * CAP, model_width), 'seq', 0)...  9.64 us
    add x7, other arithmetic, combine_states(): later[0][:, None, None] * earlier[1] + later[1]  9.08 us
    all_to_all x1, blocking collectives, on_device(): lax.all_to_all(outgoing, 'exp', split_axis=0, concat_axis=0, tiled=True)  6.58 us
  transfers between devices with their start and end apart: 6, of which 5 were waited for; matrix products, arithmetic and copies ran while one was open for 14% of the time, Pallas kernels for 0%

profile of v1, /device:TPU:31, one launch (start us, length us, event | category | flops | bytes accessed | tf_op | source)
XLA Modules:
  0.0 259.3 jit_solution(13140699687530710543)
XLA Ops:
  7.2 0.0 copy-start
  7.2 0.0 reduce-scatter.2.cloned.1.call-start
  7.2 1.0 broadcast_in_dim.21
  8.2 0.1 reshape.108
  8.3 0.8 copy.66
  9.1 0.1 reshape.107
  9.1 0.1 fusion.20
  9.3 0.2 select_reduce_fusion
  9.5 0.2 convolution_convert_fusion.1
  9.7 0.1 reshape.109
  9.7 6.6 %all_to_all.10 = bf16[4,4,6144]{2,1,0:T(4,128)(2,1)S(1)} all-to-all(bf16[4,4,6144]{2,1,0:T(4,128)(2,1)S(1)} %reshape.109), channel_id=1, replica_groups=mesh['seq'=8,'exp'=4] {'exp'}, dimensions={0} | all-to-all | bytes 393216 | tf_op jit(solution)/shard_map/all_to_all | solution.py:96
  16.4 0.3 collective-permute-start
  16.7 8.0 %collective-permute-done = bf16[16,6144]{1,0:T(8,128)(2,1)S(1)} collective-permute-done((bf16[16,6144]{1,0:T(8,128)(2,1)S(1)}, bf16[16,6144]{1,0:T(8,128)(2,1)S(1)}, u32[]{:S(2)}, u32[]{:S(2)}) %collective-permute-start) | collective-permute-done | bytes 196640 | tf_op jit(solution)/shard_map/ppermute | solution.py:16
  24.7 0.1 collective-permute-start.1
  24.8 10.6 %collective-permute-done.1 = bf16[32,6144]{1,0:T(8,128)(2,1)S(1)} collective-permute-done((bf16[32,6144]{1,0:T(8,128)(2,1)S(1)}, bf16[32,6144]{1,0:T(8,128)(2,1)S(1)}, u32[]{:S(2)}, u32[]{:S(2)}) %collective-permute-start.1) | collective-permute-done | bytes 393248 | tf_op jit(solution)/shard_map/ppermute | solution.py:16
  35.4 0.1 pad_maximum_fusion
  35.5 0.1 collective-permute-start.2
  35.6 35.7 %collective-permute-done.2 = bf16[64,6144]{1,0:T(8,128)(2,1)S(1)} collective-permute-done((bf16[64,6144]{1,0:T(8,128)(2,1)S(1)}, bf16[64,6144]{1,0:T(8,128)(2,1)S(1)}, u32[]{:S(2)}, u32[]{:S(2)}) %collective-permute-start.2) | collective-permute-done | bytes 786464 | tf_op jit(solution)/shard_map/ppermute | solution.py:16
  71.3 0.1 constant_dynamic-update-slice_fusion.4
  71.4 0.1 constant_dynamic-update-slice_fusion
  71.5 9.6 %fusion.12 = f32[128,1152]{1,0:T(8,128)S(1)} fusion(bf16[6144,1152]{0,1:T(8,128)(2,1)} %bitcast.58, bf16[256,6144]{1,0:T(8,128)(2,1)S(1)} %constant_dynamic-update-slice_fusion, s32[]{:T(128)S(6)} %select_n.26), kind=kOutput, calls=%fused_computation.20 | convolution fusion | flops 1811939328 | bytes 16318468 | tf_op jit(solution)/shard_map/dot_general | solution.py:97
  81.1 5.7 %convolution_convert_fusion = bf16[128,6144]{1,0:T(8,128)(2,1)} fusion(bf16[1,576,6144]{2,1,0:T(8,128)(2,1)} %param.17, f32[128,1152]{1,0:T(8,128)S(1)} %fusion.12), kind=kOutput, calls=%fused_computation.3 | convolution fusion | flops 907198464 | bytes 9306112 | tf_op jit(solution)/shard_map/dot_general | solution.py:104
  86.8 0.0 reduce-scatter.2.cloned.1.call-update
  86.8 0.0 all-gather.4.cloned.1.call-start
  86.9 0.0 copy-done
  86.9 1.2 reduce-window.6
  88.0 0.2 slice_reduce_fusion
  88.2 5.9 %fusion.28 = (bf16[512,1,2048]{2,0,1:T(8,128)(2,1)S(1)}, bf16[512,1,2048]{2,0,1:T(8,128)(2,1)}, bf16[512,1,2048]{2,0,1:T(8,128)(2,1)}) fusion(bf16[512,3,2048]{2,0,1:T(8,128)(2,1)} %param.10), kind=kLoop, calls=%fused_computation.59 | loop fusion | bytes 12582912 | tf_op jit(solution)/shard_map/slice | solution.py:52
  94.1 3.9 %copy.61 = bf16[512,1,2048]{0,2,1:T(8,128)(2,1)} copy(bf16[512,1,2048]{2,0,1:T(8,128)(2,1)} %get-tuple-element.59) | data formatting | bytes 4194304 | tf_op jit(solution)/shard_map/slice | solution.py:53
  98.0 2.5 copy.75
  100.5 0.1 fusion.27
  100.6 0.2 slice_reduce_fusion.1
  100.8 0.1 bitcast_exponential_fusion
  100.9 5.3 %fusion.14 = bf16[16,128,128]{2,1,0:T(8,128)(2,1)} fusion(bf16[512,16,128]{0,2,1:T(8,128)(2,1)} %bitcast.61, bf16[512,16,128]{0,2,1:T(8,128)(2,1)} %bitcast.63, f32[512,16]{0,1:T(8,128)S(1)} %get-tuple-element.61), kind=kOutput, calls=%fused_computation.22 | convolution fusion | flops 1612972032 | bytes 4751360 | tf_op jit(solution)/shard_map/thi,thj->hij/dot_general | solution.py:57
  106.2 0.0 all-gather.4.cloned.1.call-update
  106.2 2.9 %copy.74 = bf16[512,1,2048]{0,2,1:T(8,128)(2,1)S(1)} copy(bf16[512,1,2048]{2,0,1:T(8,128)(2,1)} %get-tuple-element.58) | data formatting | bytes 4194304
  109.1 0.1 iota_compare_fusion
  109.2 40.3 %reduce-scatter.2.cloned.1.call-done = bf16[16,6144]{1,0:T(8,128)(2,1)} async-done(((bf16[128,6144]{1,0:T(8,128)(2,1)}), bf16[16,6144]{1,0:T(8,128)(2,1)}) %reduce-scatter.2.cloned.1.call-update) | async-done | bytes 196624 | tf_op jit(solution)/shard_map/reduce_scatter | solution.py:103
  149.5 1.7 reshape.112
  151.2 5.7 %all-to-all-start.1 = ((bf16[4,4,6144]{2,1,0:T(4,128)(2,1)}), bf16[4,4,6144]{2,1,0:T(4,128)(2,1)S(1)}, u32[]{:S(2)}, u32[]{:S(2)}) async-start(bf16[4,4,6144]{2,1,0:T(4,128)(2,1)} %reshape.112), calls=%async_computation.2 | async-start | bytes 393216 | tf_op jit(solution)/shard_map/all_to_all | solution.py:110
  156.9 10.7 %fusion.11 = f32[16,512,128]{1,2,0:T(8,128)} fusion(bf16[512,16,128]{0,2,1:T(8,128)(2,1)} %bitcast.62, bf16[512,16,128]{0,2,1:T(8,128)(2,1)S(1)} %bitcast.59, bf16[512,16,128]{0,2,1:T(8,128)(2,1)} %bitcast.64, f32[16,512]{1,0:T(8,128)S(1)} %get-tuple-element.63, pred[512,512]{1,0:T(8,128)(4,1)S(1)} %iota_compare_fusion), kind=kOutput, calls=%fused_computation.19 | convolution fusion | flops 2164260864 | bytes 10780672 | tf_op jit(solution)/shard_map/htu,uhd->thd/dot_general | solution.py:66
  167.6 0.2 fusion.21
  167.7 13.1 %all-gather.1 = bf16[8,1,16]{2,1,0:T(2,128)(2,1)S(1)} all-gather(bf16[1,1,16]{2,1,0:T(2,128)(2,1)S(1)} %bitcast.67), channel_id=1, replica_groups=mesh['seq'=8,'exp'=4] {'seq'}, dimensions={0}, use_global_device_ids=true | all-gather | bytes 288 | tf_op jit(solution)/shard_map/all_gather | solution.py:26
  180.8 0.1 copy.67
  180.9 0.1 mul.96
  181.0 0.0 all-to-all-done.1
  181.0 0.3 convolution_multiply_fusion
  181.3 0.2 reshape.114
  181.5 1.1 reduce_sum.29
  182.7 42.6 %all-gather.4.cloned.1.call-done = bf16[128,128,128]{2,1,0:T(8,128)(2,1)} async-done(((bf16[16,128,128]{2,1,0:T(8,128)(2,1)}), bf16[128,128,128]{2,1,0:T(8,128)(2,1)}) %all-gather.4.cloned.1.call-update) | async-done | bytes 4194320 | tf_op jit(solution)/shard_map/all_gather | solution.py:26
  225.2 0.1 broadcast_in_dim.20
  225.3 9.4 %while.12 = (s32[]{:T(128)}, f32[16,128,128]{2,1,0:T(8,128)S(1)}, s32[]{:T(128)}, bf16[8,16]{1,0:T(8,128)(2,1)S(1)}, bf16[8,16,128,128]{3,2,1,0:T(8,128)(2,1)}, /*index=5*/s32[]{:T(128)}, s32[]{:T(128)}, s32[]{:T(128)}) while((s32[]{:T(128)}, f32[16,128,128]{2,1,0:T(8,128)S(1)}, s32[]{:T(128)}, bf16[8,16]{1,0:T(8,128)(2,1)S(1)}, ...), condition=%wide.region_3.4_spmd, body=%wide.region_2.3_spmd.sunk | while | flops 786453 | bytes 2621735 | solution.py:40
  225.4 1.3 convert_add_fusion.2
  226.7 1.3 convert_add_fusion.2
  228.1 1.3 convert_add_fusion.2
  229.4 1.3 convert_add_fusion.2
  230.7 1.3 convert_add_fusion.2
  232.1 1.3 convert_add_fusion.2
  233.4 1.3 convert_add_fusion.2
  234.7 5.8 %multiply_reduce_fusion = (f32[512,16]{0,1:T(8,128)S(1)}, f32[512,16,128]{0,2,1:T(8,128)S(1)}) fusion(f32[16,128,128]{2,1,0:T(8,128)S(1)} %get-tuple-element.46, bf16[512,16,128]{0,2,1:T(8,128)(2,1)S(1)} %bitcast.60, f32[512,16]{0,1:T(8,128)S(1)} %get-tuple-element.60, f32[16,512,128]{1,2,0:T(8,128)} %fusion.11), kind=kOutput, calls=%fused_computation.9 | convolution fusion | flops 1615847424 | bytes 11599872 | tf_op jit(solution)/shard_map/thd,hde->the/dot_general | solution.py:67
  240.5 2.5 broadcast_multiply_fusion
  243.0 5.4 %copy.65 = f32[512,2048]{1,0:T(8,128)} copy(f32[512,2048]{0,1:T(8,128)} %bitcast.57) | data formatting | bytes 8388608 | tf_op jit(solution)/shard_map/reshape | solution.py:75
  248.5 0.0 copy-done.2
  248.5 4.0 %multiply_convert_fusion.1 = bf16[512,2048]{1,0:T(8,128)(2,1)} fusion(f32[512,2048]{1,0:T(8,128)} %copy.65, f32[2048]{0:T(1024)S(1)} %copy-done.2), kind=kLoop, calls=%fused_computation.8 | loop fusion | flops 2097152 | bytes 6299648 | tf_op jit(solution)/shard_map/convert_element_type | solution.py:75
  (28 shorter events, 0.4 us)
Async XLA Ops:
  7.2 79.7 %copy-start = (f32[512,16]{0,1:T(8,128)S(1)}, f32[512,16]{0,1:T(8,128)}, u32[]{:S(2)}) copy-start(f32[512,16]{0,1:T(8,128)} %param.11) | copy-start | bytes 98308
  7.2 142.3 %reduce-scatter.2.cloned.1.call-start = ((), (), s32[]{:S(2)}) async-start(), calls=%async_computation.3 | async-start | bytes 1769472 | tf_op jit(solution)/shard_map/reduce_scatter | solution.py:103
  16.4 8.3 %collective-permute-start = (bf16[16,6144]{1,0:T(8,128)(2,1)S(1)}, bf16[16,6144]{1,0:T(8,128)(2,1)S(1)}, u32[]{:S(2)}, u32[]{:S(2)}) collective-permute-start(bf16[16,6144]{1,0:T(8,128)(2,1)S(1)} %reshape.110), channel_id=1, source_target_pairs={{0,28},{4,0},{8,4},{12,8},{16,12},{20,16},{24,20},{28,24},{1,29},{... | collective-permute-start | bytes 589832 | tf_op jit(solution)/shard_map/ppermute | solution.py:16
  24.7 10.7 %collective-permute-start.1 = (bf16[32,6144]{1,0:T(8,128)(2,1)S(1)}, bf16[32,6144]{1,0:T(8,128)(2,1)S(1)}, u32[]{:S(2)}, u32[]{:S(2)}) collective-permute-start(bf16[32,6144]{1,0:T(8,128)(2,1)S(1)} %pad_maximum_fusion.1), channel_id=1, source_target_pairs={{0,24},{4,28},{8,0},{12,4},{16,8},{20,12},{24,16},{28,20},{1,25},{... | collective-permute-start | bytes 1179656 | tf_op jit(solution)/shard_map/ppermute | solution.py:16
  35.5 35.8 %collective-permute-start.2 = (bf16[64,6144]{1,0:T(8,128)(2,1)S(1)}, bf16[64,6144]{1,0:T(8,128)(2,1)S(1)}, u32[]{:S(2)}, u32[]{:S(2)}) collective-permute-start(bf16[64,6144]{1,0:T(8,128)(2,1)S(1)} %pad_maximum_fusion), channel_id=1, source_target_pairs={{0,16},{4,20},{8,24},{12,28},{16,0},{20,4},{24,8},{28,12},{1,17},{... | collective-permute-start | bytes 2359304 | tf_op jit(solution)/shard_map/ppermute | solution.py:16
  86.8 138.4 %all-gather.4.cloned.1.call-start = ((), (), s32[]{:S(2)}) async-start(), calls=%async_computation.4 | async-start | bytes 4718592 | tf_op jit(solution)/shard_map/all_gather | solution.py:26
  151.2 29.8 %all-to-all-start.1 = ((bf16[4,4,6144]{2,1,0:T(4,128)(2,1)}), bf16[4,4,6144]{2,1,0:T(4,128)(2,1)S(1)}, u32[]{:S(2)}, u32[]{:S(2)}) async-start(bf16[4,4,6144]{2,1,0:T(4,128)(2,1)} %reshape.112), calls=%async_computation.2 | async-start | bytes 393216 | tf_op jit(solution)/shard_map/all_to_all | solution.py:110
  156.9 23.9 %copy-start.3 = (f32[8,2]{0,1:T(2,128)S(1)}, f32[8,2]{0,1:T(2,128)}, u32[]{:S(2)}) copy-start(f32[8,2]{0,1:T(2,128)} %param.15) | copy-start | bytes 196
  243.0 5.4 %copy-start.2 = (f32[2048]{0:T(1024)S(1)}, f32[2048]{0:T(1024)}, u32[]{:S(2)}) copy-start(f32[2048]{0:T(1024)} %param.12) | copy-start | bytes 24580
  243.0 9.4 %copy-start.1 = (f32[512,16]{0,1:T(8,128)S(1)}, f32[512,16]{0,1:T(8,128)}, u32[]{:S(2)}) copy-start(f32[512,16]{0,1:T(8,128)} %param.11) | copy-start | bytes 98308
Sparse Core Ops, SparseCore 0:
  86.9 62.5 reduce-scatter.1
  151.8 73.3 all-gather.3
